TPU v7x, 128 devices: a whole 4x4x4 slice. The times are simulated.
128 devices in a mesh: group: 4 (over y_lo, core), mp: 32 (over z, x, y_hi).
Axes of the slice: x: 4, y: 4 (y_hi: 2, y_lo: 2; y = y_hi * 2 + y_lo), z: 4, core: 2. Of those that a mesh axis runs over, the one named last changes fastest.
Arguments:
- tokens: bfloat16 [5120, 2048], P(('group', 'mp')), may hold values from -6 to 6
- lengths: int32 [4, 8], P('group'), may hold values from 1 to 512, 1280 in all within a row
- query_gain: float32 [2048], replicated, may hold values from 0.5 to 8
- key_gain: float32 [2048], replicated, may hold values from 0.5 to 8
- attn_post_gain: float32 [2048], replicated, may hold values from 0.5 to 1.5
- mlp_post_gain: float32 [2048], replicated, may hold values from 0.5 to 1.5
- query_weight: float32 [2048, 2048], P(('mp', 'group')), may hold values from -4 to 4
- key_weight: float32 [2048, 2048], P(('mp', 'group')), may hold values from -4 to 4
- value_weight: float32 [2048, 2048], P(('mp', 'group')), may hold values from -0.125 to 0.125
- output_weight: float32 [2048, 2048], P(('mp', 'group')), may hold values from -0.125 to 0.125
- gate_weight: float32 [2048, 8192], P(('mp', 'group')), may hold values from -0.125 to 0.125
- up_weight: float32 [2048, 8192], P(('mp', 'group')), may hold values from -0.125 to 0.125
- down_weight: float32 [8192, 2048], P(('mp', 'group')), may hold values from -0.0625 to 0.0625
Outputs:
- layer_out: bfloat16 [5120, 2048], P(('group', 'mp'))
Inputs may be any that keep to these rules, and one draw needn't show every extreme that they name: In each group the 8 prompt lengths sum to 1280; the longest is exactly 512.
All inputs are finite; a program needn't handle non-finite values.
Results may differ from a plain program's by a relative error of at most 0.034.
Values may be sent and summed in bfloat16 or wider, within the bound.
A program may use at most 64 MiB of HBM per device.

v0:
```python
import math
import jax
import jax.numpy as jnp
from jax import lax
from jax.sharding import PartitionSpec as P

HEAD_DIM = 128
NORM_EPSILON = 1e-06
ROPE_BASE = 500000.0


def partner_2(block, axis, apart):
    count = lax.axis_size(axis)
    route = []
    for low in range(count):
        high = low | 1 << apart
        if high != low and high < count:
            route += [(low, high), (high, low)]
    return lax.ppermute(block, axis, route)


def token_layout(prompt_lens, row_count):
    seg_ends = jnp.cumsum(prompt_lens)
    starts = seg_ends - prompt_lens
    indices = jnp.arange(row_count, dtype=jnp.int32)
    segment = jnp.sum((indices[:, None] >= seg_ends[None, :]).astype(jnp.int32), axis=1)
    member = segment[:, None] == jnp.arange(prompt_lens.shape[0], dtype=jnp.int32)[None, :]
    opening = jnp.sum(jnp.where(member, starts[None, :], 0), axis=1)
    return (segment, indices - opening)


def rotary(head_values, position, head_size):
    half_size = head_size // 2
    frequency = jnp.exp(
        jnp.arange(half_size, dtype=jnp.float32) * (-2.0 * math.log(ROPE_BASE) / head_size)
    )
    angles = position.astype(jnp.float32)[:, None] * frequency[None, :]
    cosines = jnp.cos(angles)
    sines = jnp.sin(angles)
    front_half = head_values[..., :half_size]
    back_half = head_values[..., half_size:]
    return jnp.concatenate(
        [front_half * cosines - back_half * sines, back_half * cosines + front_half * sines],
        axis=-1,
    )


def head_attention(queries, query_rows, keys_rot, values_h, segment, head_size):
    scores = lax.dot_general(
        queries, keys_rot, (((1,), (1,)), ((), ())), preferred_element_type=jnp.float32
    )
    scores = scores * (1.0 / math.sqrt(head_size))
    key_rows = jnp.arange(keys_rot.shape[0], dtype=jnp.int32)
    query_segment = jnp.take(segment, query_rows)
    allowed = (query_segment[:, None] == segment[None, :]) & (
        key_rows[None, :] <= query_rows[:, None]
    )
    scores = jnp.where(allowed, scores, -1e30)
    row_max = jnp.max(scores, axis=1, keepdims=True)
    weights = jnp.exp(scores - row_max)
    weights = weights / jnp.sum(weights, axis=1, keepdims=True)
    probabilities = weights.astype(jnp.bfloat16)
    return jnp.dot(probabilities, values_h, preferred_element_type=jnp.float32).astype(jnp.bfloat16)


def rms_scale(values_in, gain):
    return (
        values_in
        * lax.rsqrt(jnp.mean(values_in * values_in, axis=-1, keepdims=True) + NORM_EPSILON)
        * gain
    )


def per_device(
    tokens,
    lengths,
    query_gain,
    key_gain,
    attn_post_gain,
    mlp_post_gain,
    query_weight,
    key_weight,
    value_weight,
    output_weight,
    gate_weight,
    up_weight,
    down_weight,
):
    features = tokens.shape[1]
    shards = lax.axis_size("mp")
    my_index = lax.axis_index("mp")
    col_width = features // shards
    tok_rows = tokens.shape[0]
    group_rows = tok_rows * shards
    stack_attn = jnp.stack([query_weight, key_weight, value_weight]).astype(jnp.bfloat16)
    stack_mlp = jnp.stack([gate_weight, up_weight]).astype(jnp.bfloat16)
    down_piece = down_weight.astype(jnp.bfloat16)[None]
    output_piece = output_weight.astype(jnp.bfloat16)[None]
    attn_rows, mlp_rows, down_rows, output_rows = (
        lax.all_gather(stack_attn, "group", axis=1, tiled=True),
        lax.all_gather(stack_mlp, "group", axis=1, tiled=True),
        lax.all_gather(down_piece, "group", axis=1, tiled=True),
        lax.all_gather(output_piece, "group", axis=1, tiled=True),
    )
    attn_block, mlp_block = (
        lax.all_to_all(attn_rows, "mp", split_axis=2, concat_axis=1, tiled=True),
        lax.all_to_all(mlp_rows, "mp", split_axis=2, concat_axis=1, tiled=True),
    )
    down_block = down_rows[0]
    output_block = output_rows[0]
    parity = my_index % 2
    partner = partner_2(attn_block, "mp", 0)
    attn_block = jnp.where(
        parity == 0,
        jnp.concatenate([attn_block, partner], axis=2),
        jnp.concatenate([partner, attn_block], axis=2),
    )
    head_cols = attn_block.shape[2]
    col_start = my_index * col_width // HEAD_DIM * HEAD_DIM
    share_part = col_width / head_cols
    projected = jnp.einsum(
        "td,kdc->ktc",
        lax.all_gather(tokens, "mp", axis=0, tiled=True),
        attn_block,
        preferred_element_type=jnp.float32,
    )
    query_sq = jnp.sum(projected[0] * projected[0], axis=1) * share_part
    key_sq = jnp.sum(projected[1] * projected[1], axis=1) * share_part
    query_total, key_total = lax.psum((query_sq, key_sq), "mp")
    query_part = lax.dynamic_slice_in_dim(query_gain, col_start, head_cols)
    key_part = lax.dynamic_slice_in_dim(key_gain, col_start, head_cols)
    q_normed = projected[0] * lax.rsqrt(query_total / features + NORM_EPSILON)[:, None] * query_part
    k_normed = projected[1] * lax.rsqrt(key_total / features + NORM_EPSILON)[:, None] * key_part
    segment, position = token_layout(lengths[0], group_rows)
    local_heads = head_cols // HEAD_DIM

    def heads_first(flat):
        return flat.reshape(group_rows, local_heads, HEAD_DIM).transpose(1, 0, 2)

    queries = rotary(heads_first(q_normed), position, HEAD_DIM).astype(jnp.bfloat16)
    keys_rot = rotary(heads_first(k_normed), position, HEAD_DIM).astype(jnp.bfloat16)
    values_h = heads_first(projected[2].astype(jnp.bfloat16))
    all_rows = jnp.arange(group_rows, dtype=jnp.int32)

    def per_head(triple):
        return head_attention(triple[0], all_rows, triple[1], triple[2], segment, HEAD_DIM)

    attended = lax.map(per_head, (queries, keys_rot, values_h))
    attended = attended.transpose(1, 0, 2).reshape(group_rows, head_cols)
    attended = lax.dynamic_slice_in_dim(attended, parity * col_width, col_width, 1)
    rows_part = attended
    attn_out = lax.psum_scatter(
        jnp.dot(rows_part, output_block, preferred_element_type=jnp.float32).astype(jnp.bfloat16),
        "mp",
        scatter_dimension=0,
        tiled=True,
    ).astype(jnp.float32)
    hidden = (tokens.astype(jnp.float32) + rms_scale(attn_out, attn_post_gain)).astype(jnp.bfloat16)
    hidden_width = mlp_block.shape[2]
    mlp_weights = jnp.concatenate([mlp_block[0], mlp_block[1]], axis=1)
    both_proj = jnp.dot(
        lax.all_gather(hidden, "mp", axis=0, tiled=True),
        mlp_weights,
        preferred_element_type=jnp.float32,
    )
    activated = (jax.nn.silu(both_proj[:, :hidden_width]) * both_proj[:, hidden_width:]).astype(
        jnp.bfloat16
    )
    rows_part = activated
    mlp_out = lax.psum_scatter(
        jnp.dot(rows_part, down_block, preferred_element_type=jnp.float32).astype(jnp.bfloat16),
        "mp",
        scatter_dimension=0,
        tiled=True,
    ).astype(jnp.float32)
    return (hidden.astype(jnp.float32) + rms_scale(mlp_out, mlp_post_gain)).astype(jnp.bfloat16)


def solution(mesh):
    return jax.shard_map(
        per_device,
        mesh=mesh,
        in_specs=(
            P(("group", "mp"), None),
            P("group", None),
            P(),
            P(),
            P(),
            P(),
            P(("mp", "group"), None),
            P(("mp", "group"), None),
            P(("mp", "group"), None),
            P(("mp", "group"), None),
            P(("mp", "group"), None),
            P(("mp", "group"), None),
            P(("mp", "group"), None),
        ),
        out_specs=P(("group", "mp"), None),
        check_vma=False,
    )
```

profile of v0, /device:TPU:0, one launch (start us, length us, event | category | flops | bytes accessed | tf_op | source)
XLA Modules:
  0.0 826.0 jit_solution(16544474879725775960)
XLA Ops:
  10.0 8.8 %all_gather.18 = bf16[3,64,2048]{2,1,0:T(8,128)(2,1)S(1)} all-gather(bf16[3,16,2048]{2,1,0:T(8,128)(2,1)S(1)} %pad_maximum_fusion.1), channel_id=1, replica_groups=mesh['group'=4,'mp'=32] {'group'}, dimensions={1}, use_global_device_ids=true | all-gather | bytes 983040 | tf_op jit(solution)/shard_map/all_gather | solution.py:100
  20.2 2.5 reshape.221
  22.6 10.5 %all-to-all-start = ((bf16[32,2,6144]{2,1,0:T(2,128)(2,1)}), bf16[32,2,6144]{2,1,0:T(2,128)(2,1)S(1)}, u32[]{:S(2)}, u32[]{:S(2)}) async-start(bf16[32,2,6144]{2,1,0:T(2,128)(2,1)} %reshape.221), calls=%async_computation | async-start | bytes 1572864 | tf_op jit(solution)/shard_map/all_to_all | solution.py:106
  35.0 7.1 gather_fusion
  42.1 5.8 all-gather
  51.6 2.5 copy.35
  54.1 2.8 all_to_all.27
  58.0 20.9 %collective-permute-done = bf16[3,2048,64]{1,2,0:T(8,128)(2,1)S(1)} collective-permute-done((bf16[3,2048,64]{1,2,0:T(8,128)(2,1)S(1)}, bf16[3,2048,64]{1,2,0:T(8,128)(2,1)S(1)}, u32[]{:S(2)}, u32[]{:S(2)}) %collective-permute-start) | collective-permute-done | bytes 786464 | tf_op jit(solution)/shard_map/ppermute | solution.py:19
  79.9 24.5 %all-gather.7.cloned.1.call-done = bf16[1280,2048]{1,0:T(8,128)(2,1)} async-done(((bf16[40,2048]{1,0:T(8,128)(2,1)}), bf16[1280,2048]{1,0:T(8,128)(2,1)}) %all-gather.7.cloned.1.call-update) | async-done | bytes 5242896 | tf_op jit(solution)/shard_map/all_gather | solution.py:123
  104.3 5.2 fusion.6
  109.7 181.7 %all-reduce = (f32[1280]{0:T(1024)S(1)}, f32[1280]{0:T(1024)S(1)}) all-reduce(f32[1280]{0:T(1024)S(1)} %broadcast_multiply_fusion.1, f32[1280]{0:T(1024)S(1)} %broadcast_multiply_fusion), channel_id=1, replica_groups=mesh['group'=4,'mp'=32] {'mp'}, use_global_device_ids=true, to_apply=%region_3.4 | all-reduce | flops 2560 | bytes 20480 | tf_op jit(solution)/shard_map/psum | solution.py:129
  296.9 3.9 convolution_convert_fusion.1
  303.0 195.8 %reduce-scatter.3.cloned.1.call-done = bf16[40,2048]{1,0:T(8,128)(2,1)} async-done(((bf16[1280,2048]{1,0:T(8,128)(2,1)}), bf16[40,2048]{1,0:T(8,128)(2,1)}) %reduce-scatter.3.cloned.1.call-update) | async-done | bytes 163856 | tf_op jit(solution)/shard_map/reduce_scatter | solution.py:152
  501.6 9.6 %copy.36 = bf16[2,64,8192]{1,0,2:T(2,128)(2,1)} copy(bf16[2,64,8192]{2,1,0:T(8,128)(2,1)} %all-gather.11.cloned.1.call-done) | data formatting | bytes 4194304 | tf_op jit(solution)/shard_map/all_gather | solution.py:101
  511.1 9.8 %reshape.223 = bf16[32,2,16384]{2,1,0:T(2,128)(2,1)} reshape(bf16[8192,2,64]{2,1,0:T(2,128)(2,1)} %bitcast.54) | data formatting | bytes 4194304
  521.0 4.9 all-to-all-start.1
  527.0 22.9 %all-to-all-done.1 = bf16[32,2,16384]{2,1,0:T(2,128)(2,1)S(1)} async-done(((bf16[32,2,16384]{2,1,0:T(2,128)(2,1)}), bf16[32,2,16384]{2,1,0:T(2,128)(2,1)S(1)}, u32[]{:S(2)}, u32[]{:S(2)}) %all-to-all-start.1) | async-done | bytes 2097184 | tf_op jit(solution)/shard_map/all_to_all | solution.py:107
  549.9 4.0 reshape.224
  554.0 6.4 copy.40
  561.7 32.2 %all-gather.9.cloned.1.call-done = bf16[1280,2048]{1,0:T(8,128)(2,1)} async-done(((bf16[40,2048]{1,0:T(8,128)(2,1)}), bf16[1280,2048]{1,0:T(8,128)(2,1)}) %all-gather.9.cloned.1.call-update) | async-done | bytes 5242896 | tf_op jit(solution)/shard_map/all_gather | solution.py:162
  593.9 6.9 fusion.9
  600.7 12.4 %all-gather.13.cloned.1.call-done = bf16[256,2048]{1,0:T(8,128)(2,1)} async-done(((bf16[64,2048]{1,0:T(8,128)(2,1)}), bf16[256,2048]{1,0:T(8,128)(2,1)}) %all-gather.13.cloned.1.call-update) | async-done | bytes 1048592 | tf_op jit(solution)/shard_map/all_gather | solution.py:102
  613.2 5.9 convolution_convert_fusion
  619.1 196.5 %reduce-scatter.5.cloned.1.call-done = bf16[40,2048]{1,0:T(8,128)(2,1)} async-done(((bf16[1280,2048]{1,0:T(8,128)(2,1)}), bf16[40,2048]{1,0:T(8,128)(2,1)}) %reduce-scatter.5.cloned.1.call-update) | async-done | bytes 163856 | tf_op jit(solution)/shard_map/reduce_scatter | solution.py:170
  (74 shorter events, 27.4 us)
Async XLA Ops:
  7.4 97.0 %all-gather.7.cloned.1.call-start = ((), (), s32[]{:S(2)}) async-start(), calls=%async_computation.4 | async-start | bytes 5406720 | tf_op jit(solution)/shard_map/all_gather | solution.py:123
  18.8 15.9 %copy-start.9 = (s32[1,8]{1,0:T(1,128)S(1)}, s32[1,8]{1,0:T(1,128)}, u32[]{:S(2)}) copy-start(s32[1,8]{1,0:T(1,128)} %param.14) | copy-start | bytes 100
  18.8 16.1 %copy-start.5 = (f32[16,2048]{1,0:T(8,128)S(1)}, f32[16,2048]{1,0:T(8,128)}, u32[]{:S(2)}) copy-start(f32[16,2048]{1,0:T(8,128)} %param.22) | copy-start | bytes 393220
  22.6 27.7 %all-to-all-start = ((bf16[32,2,6144]{2,1,0:T(2,128)(2,1)}), bf16[32,2,6144]{2,1,0:T(2,128)(2,1)S(1)}, u32[]{:S(2)}, u32[]{:S(2)}) async-start(bf16[32,2,6144]{2,1,0:T(2,128)(2,1)} %reshape.221), calls=%async_computation | async-start | bytes 1572864 | tf_op jit(solution)/shard_map/all_to_all | solution.py:106
  33.1 465.6 %reduce-scatter.3.cloned.1.call-start = ((), (), s32[]{:S(2)}) async-start(), calls=%async_computation.5 | async-start | bytes 5406720 | tf_op jit(solution)/shard_map/reduce_scatter | solution.py:152
  56.9 22.1 %collective-permute-start = (bf16[3,2048,64]{1,2,0:T(8,128)(2,1)S(1)}, bf16[3,2048,64]{1,2,0:T(8,128)(2,1)S(1)}, u32[]{:S(2)}, u32[]{:S(2)}) collective-permute-start(bf16[3,2048,64]{1,2,0:T(8,128)(2,1)S(1)} %all_to_all.27), channel_id=1, source_target_pairs={{0,1},{1,0},{2,3},{3,2},{4,5},{5,4},{6,7},{7,6},{8,9},{9,8},{10,11... | collective-permute-start | bytes 2359304 | tf_op jit(solution)/shard_map/ppermute | solution.py:19
  78.9 0.9 copy-start.8
  300.8 1.0 copy-start.2
  300.8 1.2 copy-start.3
  300.8 199.0 %copy-start.1 = (bf16[40,2048]{1,0:T(8,128)(2,1)S(1)}, bf16[40,2048]{1,0:T(8,128)(2,1)}, u32[]{:S(2)}) copy-start(bf16[40,2048]{1,0:T(8,128)(2,1)} %param.13) | copy-start | bytes 491524
  300.8 199.0 %copy-start.6 = (f32[2048]{0:T(1024)S(1)}, f32[2048]{0:T(1024)}, u32[]{:S(2)}) copy-start(f32[2048]{0:T(1024)} %param.17) | copy-start | bytes 24580
  300.8 200.8 %all-gather.11.cloned.1.call-start = ((), (), s32[]{:S(2)}) async-start(), calls=%async_computation.7 | async-start | bytes 2621440 | tf_op jit(solution)/shard_map/all_gather | solution.py:101
  302.9 291.0 %all-gather.9.cloned.1.call-start = ((), (), s32[]{:S(2)}) async-start(), calls=%async_computation.6 | async-start | bytes 5406720 | tf_op jit(solution)/shard_map/all_gather | solution.py:162
  521.0 5.0 copy-start.4
  521.0 29.0 %all-to-all-start.1 = ((bf16[32,2,16384]{2,1,0:T(2,128)(2,1)}), bf16[32,2,16384]{2,1,0:T(2,128)(2,1)S(1)}, u32[]{:S(2)}, u32[]{:S(2)}) async-start(bf16[32,2,16384]{2,1,0:T(2,128)(2,1)} %reshape.223), calls=%async_computation.2 | async-start | bytes 4194304 | tf_op jit(solution)/shard_map/all_to_all | solution.py:107
  525.9 87.3 %all-gather.13.cloned.1.call-start = ((), (), s32[]{:S(2)}) async-start(), calls=%async_computation.9 | async-start | bytes 1310720 | tf_op jit(solution)/shard_map/all_gather | solution.py:102
  526.7 288.8 %reduce-scatter.5.cloned.1.call-start = ((), (), s32[]{:S(2)}) async-start(), calls=%async_computation.8 | async-start | bytes 5406720 | tf_op jit(solution)/shard_map/reduce_scatter | solution.py:170
  619.1 197.6 %copy-start = (bf16[40,2048]{1,0:T(8,128)(2,1)S(1)}, bf16[40,2048]{1,0:T(8,128)(2,1)}, u32[]{:S(2)}) copy-start(bf16[40,2048]{1,0:T(8,128)(2,1)} %fusion.33) | copy-start | bytes 491524
  619.1 197.6 %copy-start.7 = (f32[2048]{0:T(1024)S(1)}, f32[2048]{0:T(1024)}, u32[]{:S(2)}) copy-start(f32[2048]{0:T(1024)} %param.18) | copy-start | bytes 24580
Sparse Core Ops, SparseCore 0:
  11.3 93.0 all-gather.6
  300.9 197.7 reduce-scatter.2
Sparse Core Ops, SparseCore 1:
  303.0 30.8 all-gather.10
  501.6 92.2 all-gather.8
  595.4 17.7 all-gather.12
  619.2 196.3 reduce-scatter.4
where the time goes:
time: 827 us; the launch traced here: 826 us
  waiting for transfers between devices  508 us (61%)
  blocking collectives  196 us (24%)
  local copies, waits for them, and re-layouts  52.2 us (6%)
  matrix products  24.7 us (3%)
  starting transfers between devices  16.9 us (2%)
  between operations  15.4 us (2%)
  other arithmetic  12.3 us (1%)
    reduce_scatter x1, waiting for transfers between devices, per_device(): lax.psum_scatter(jnp.dot(rows_part, down_block, preferred_element_type=jn...  196 us
    reduce_scatter x1, waiting for transfers between devices, per_device(): lax.psum_scatter(jnp.dot(rows_part, output_block, preferred_element_type=...  196 us
    psum x1, blocking collectives, per_device(): query_total, key_total = lax.psum((query_sq, key_sq), 'mp')  182 us
    all_gather x1, waiting for transfers between devices, per_device(): lax.all_gather(hidden, 'mp', axis=0, tiled=True)  32.2 us
    all_gather x1, waiting for transfers between devices, per_device(): lax.all_gather(tokens, 'mp', axis=0, tiled=True)  24.5 us
    all_to_all x1, waiting for transfers between devices, per_device(): lax.all_to_all(mlp_rows, 'mp', split_axis=2, concat_axis=1, tiled=True)  22.9 us
    ppermute x1, waiting for transfers between devices, partner_2(): return lax.ppermute(block, axis, route)  20.9 us
    unnamed x24, local copies, waits for them, and re-layouts  19.6 us
  transfers between devices with their start and end apart: 9, of which 8 were waited for; matrix products, arithmetic and copies ran while one was open for 7% of the time, Pallas kernels for 0%

commit v1 on v0

--- a/solution.py
+++ b/solution.py
@@ -103,7 +103,12 @@
         lax.all_gather(output_piece, "group", axis=1, tiled=True),
     )
     attn_block, mlp_block = (
-        lax.all_to_all(attn_rows, "mp", split_axis=2, concat_axis=1, tiled=True),
+        jnp.concatenate(
+            lax.all_to_all(
+                jnp.stack(jnp.split(attn_rows, lax.axis_size("mp"), axis=2)), "mp", 0, 0
+            ),
+            axis=1,
+        ),
         lax.all_to_all(mlp_rows, "mp", split_axis=2, concat_axis=1, tiled=True),
     )
     down_block = down_rows[0]

time: 827 us -> 826 us (level)
    unnamed x24 -> x57, local copies, waits for them, and re-layouts: 19.6 us -> 20.7 us
where the time goes in v1:
time: 826 us; the launch traced here: 825 us
  waiting for transfers between devices  511 us (62%)
  blocking collectives  194 us (23%)
  local copies, waits for them, and re-layouts  49.4 us (6%)
  matrix products  25.2 us (3%)
  starting transfers between devices  17.4 us (2%)
  between operations  15.4 us (2%)
  other arithmetic  12.3 us (1%)
    reduce_scatter x1, waiting for transfers between devices, per_device(): lax.psum_scatter(jnp.dot(rows_part, down_block, preferred_element_type=jn...  197 us
    reduce_scatter x1, waiting for transfers between devices, per_device(): lax.psum_scatter(jnp.dot(rows_part, output_block, preferred_element_type=...  196 us
    psum x1, blocking collectives, per_device(): query_total, key_total = lax.psum((query_sq, key_sq), 'mp')  179 us
    all_gather x1, waiting for transfers between devices, per_device(): lax.all_gather(hidden, 'mp', axis=0, tiled=True)  31 us
    all_gather x1, waiting for transfers between devices, per_device(): lax.all_gather(tokens, 'mp', axis=0, tiled=True)  28.9 us
    all_to_all x1, waiting for transfers between devices, per_device(): lax.all_to_all(mlp_rows, 'mp', split_axis=2, concat_axis=1, tiled=True)  23.3 us
    unnamed x57, local copies, waits for them, and re-layouts  20.7 us
    ppermute x1, waiting for transfers between devices, partner_2(): return lax.ppermute(block, axis, route)  18.7 us
  transfers between devices with their start and end apart: 9, of which 8 were waited for; matrix products, arithmetic and copies ran while one was open for 7% of the time, Pallas kernels for 0%

profile of v1, /device:TPU:0, one launch (start us, length us, event | category | flops | bytes accessed | tf_op | source)
XLA Modules:
  0.0 824.6 jit_solution(5793490338654956942)
XLA Ops:
  10.0 8.8 %all_gather.18 = bf16[3,64,2048]{2,1,0:T(8,128)(2,1)S(1)} all-gather(bf16[3,16,2048]{2,1,0:T(8,128)(2,1)S(1)} %pad_maximum_fusion.1), channel_id=1, replica_groups=mesh['group'=4,'mp'=32] {'group'}, dimensions={1}, use_global_device_ids=true | all-gather | bytes 983040 | tf_op jit(solution)/shard_map/all_gather | solution.py:100
  20.8 1.9 reshape.229
  22.7 10.5 %all-to-all-start = ((bf16[32,2,6144]{2,1,0:T(2,128)(2,1)}), bf16[32,2,6144]{2,1,0:T(2,128)(2,1)S(1)}, u32[]{:S(2)}, u32[]{:S(2)}) async-start(bf16[32,2,6144]{2,1,0:T(2,128)(2,1)} %reshape.229), calls=%async_computation | async-start | bytes 1572864 | tf_op jit(solution)/shard_map/all_to_all | solution.py:107
  35.1 7.1 gather_fusion
  42.2 5.8 all-gather
  48.0 2.3 all-to-all-done
  55.3 18.7 %collective-permute-done = bf16[3,2048,64]{1,2,0:T(8,128)(2,1)S(1)} collective-permute-done((bf16[3,2048,64]{1,2,0:T(8,128)(2,1)S(1)}, bf16[3,2048,64]{1,2,0:T(8,128)(2,1)S(1)}, u32[]{:S(2)}, u32[]{:S(2)}) %collective-permute-start) | collective-permute-done | bytes 786464 | tf_op jit(solution)/shard_map/ppermute | solution.py:19
  74.9 28.9 %all-gather.7.cloned.1.call-done = bf16[1280,2048]{1,0:T(8,128)(2,1)} async-done(((bf16[40,2048]{1,0:T(8,128)(2,1)}), bf16[1280,2048]{1,0:T(8,128)(2,1)}) %all-gather.7.cloned.1.call-update) | async-done | bytes 5242896 | tf_op jit(solution)/shard_map/all_gather | solution.py:128
  103.8 5.7 fusion.6
  109.6 179.4 %all-reduce = (f32[1280]{0:T(1024)S(1)}, f32[1280]{0:T(1024)S(1)}) all-reduce(f32[1280]{0:T(1024)S(1)} %broadcast_multiply_fusion.1, f32[1280]{0:T(1024)S(1)} %broadcast_multiply_fusion), channel_id=1, replica_groups=mesh['group'=4,'mp'=32] {'mp'}, use_global_device_ids=true, to_apply=%region_3.4 | all-reduce | flops 2560 | bytes 20480 | tf_op jit(solution)/shard_map/psum | solution.py:134
  294.5 3.9 convolution_convert_fusion.1
  300.6 196.5 %reduce-scatter.3.cloned.1.call-done = bf16[40,2048]{1,0:T(8,128)(2,1)} async-done(((bf16[1280,2048]{1,0:T(8,128)(2,1)}), bf16[40,2048]{1,0:T(8,128)(2,1)}) %reduce-scatter.3.cloned.1.call-update) | async-done | bytes 163856 | tf_op jit(solution)/shard_map/reduce_scatter | solution.py:157
  499.9 9.5 %copy.30 = bf16[2,64,8192]{1,0,2:T(2,128)(2,1)} copy(bf16[2,64,8192]{2,1,0:T(8,128)(2,1)} %all-gather.11.cloned.1.call-done) | data formatting | bytes 4194304 | tf_op jit(solution)/shard_map/all_gather | solution.py:101
  509.5 9.8 %reshape.231 = bf16[32,2,16384]{2,1,0:T(2,128)(2,1)} reshape(bf16[8192,2,64]{2,1,0:T(2,128)(2,1)} %bitcast.178) | data formatting | bytes 4194304
  519.3 5.5 all-to-all-start.1
  525.9 23.3 %all-to-all-done.1 = bf16[32,2,16384]{2,1,0:T(2,128)(2,1)S(1)} async-done(((bf16[32,2,16384]{2,1,0:T(2,128)(2,1)}), bf16[32,2,16384]{2,1,0:T(2,128)(2,1)S(1)}, u32[]{:S(2)}, u32[]{:S(2)}) %all-to-all-start.1) | async-done | bytes 2097184 | tf_op jit(solution)/shard_map/all_to_all | solution.py:112
  549.1 4.0 reshape.232
  553.2 6.4 copy.34
  560.9 31.0 %all-gather.9.cloned.1.call-done = bf16[1280,2048]{1,0:T(8,128)(2,1)} async-done(((bf16[40,2048]{1,0:T(8,128)(2,1)}), bf16[1280,2048]{1,0:T(8,128)(2,1)}) %all-gather.9.cloned.1.call-update) | async-done | bytes 5242896 | tf_op jit(solution)/shard_map/all_gather | solution.py:167
  592.0 6.9 fusion.9
  598.8 12.4 %all-gather.13.cloned.1.call-done = bf16[256,2048]{1,0:T(8,128)(2,1)} async-done(((bf16[64,2048]{1,0:T(8,128)(2,1)}), bf16[256,2048]{1,0:T(8,128)(2,1)}) %all-gather.13.cloned.1.call-update) | async-done | bytes 1048592 | tf_op jit(solution)/shard_map/all_gather | solution.py:102
  611.3 5.9 convolution_convert_fusion
  617.2 197.0 %reduce-scatter.5.cloned.1.call-done = bf16[40,2048]{1,0:T(8,128)(2,1)} async-done(((bf16[1280,2048]{1,0:T(8,128)(2,1)}), bf16[40,2048]{1,0:T(8,128)(2,1)}) %reduce-scatter.5.cloned.1.call-update) | async-done | bytes 163856 | tf_op jit(solution)/shard_map/reduce_scatter | solution.py:175
  815.3 1.7 fusion.37
  (107 shorter events, 26.3 us)
Async XLA Ops:
  7.4 96.4 %all-gather.7.cloned.1.call-start = ((), (), s32[]{:S(2)}) async-start(), calls=%async_computation.4 | async-start | bytes 5406720 | tf_op jit(solution)/shard_map/all_gather | solution.py:128
  20.8 14.0 %copy-start.10 = (s32[1,8]{1,0:T(1,128)S(1)}, s32[1,8]{1,0:T(1,128)}, u32[]{:S(2)}) copy-start(s32[1,8]{1,0:T(1,128)} %param.14) | copy-start | bytes 100
  20.8 14.2 %copy-start.6 = (f32[16,2048]{1,0:T(8,128)S(1)}, f32[16,2048]{1,0:T(8,128)}, u32[]{:S(2)}) copy-start(f32[16,2048]{1,0:T(8,128)} %param.22) | copy-start | bytes 393220
  22.7 27.7 %all-to-all-start = ((bf16[32,2,6144]{2,1,0:T(2,128)(2,1)}), bf16[32,2,6144]{2,1,0:T(2,128)(2,1)S(1)}, u32[]{:S(2)}, u32[]{:S(2)}) async-start(bf16[32,2,6144]{2,1,0:T(2,128)(2,1)} %reshape.229), calls=%async_computation | async-start | bytes 1572864 | tf_op jit(solution)/shard_map/all_to_all | solution.py:107
  33.2 463.9 %reduce-scatter.3.cloned.1.call-start = ((), (), s32[]{:S(2)}) async-start(), calls=%async_computation.5 | async-start | bytes 5406720 | tf_op jit(solution)/shard_map/reduce_scatter | solution.py:157
  54.1 19.9 %copy-start.1 = (bf16[3,2048,64]{1,2,0:T(8,128)(2,1)}, bf16[3,2048,64]{1,2,0:T(8,128)(2,1)S(1)}, u32[]{:S(2)}) copy-start(bf16[3,2048,64]{1,2,0:T(8,128)(2,1)S(1)} %reshape.214) | copy-start | bytes 2359300
  54.1 19.9 %collective-permute-start = (bf16[3,2048,64]{1,2,0:T(8,128)(2,1)S(1)}, bf16[3,2048,64]{1,2,0:T(8,128)(2,1)S(1)}, u32[]{:S(2)}, u32[]{:S(2)}) collective-permute-start(bf16[3,2048,64]{1,2,0:T(8,128)(2,1)S(1)} %reshape.214), channel_id=1, source_target_pairs={{0,1},{1,0},{2,3},{3,2},{4,5},{5,4},{6,7},{7,6},{8,9},{9,8},{10,11... | collective-permute-start | bytes 2359304 | tf_op jit(solution)/shard_map/ppermute | solution.py:19
  74.0 0.9 copy-start.9
  298.4 1.0 copy-start.3
  298.4 1.2 copy-start.4
  298.4 199.7 %copy-start.2 = (bf16[40,2048]{1,0:T(8,128)(2,1)S(1)}, bf16[40,2048]{1,0:T(8,128)(2,1)}, u32[]{:S(2)}) copy-start(bf16[40,2048]{1,0:T(8,128)(2,1)} %param.13) | copy-start | bytes 491524
  298.4 199.7 %copy-start.7 = (f32[2048]{0:T(1024)S(1)}, f32[2048]{0:T(1024)}, u32[]{:S(2)}) copy-start(f32[2048]{0:T(1024)} %param.17) | copy-start | bytes 24580
  298.5 201.5 %all-gather.11.cloned.1.call-start = ((), (), s32[]{:S(2)}) async-start(), calls=%async_computation.7 | async-start | bytes 2621440 | tf_op jit(solution)/shard_map/all_gather | solution.py:101
  300.5 291.4 %all-gather.9.cloned.1.call-start = ((), (), s32[]{:S(2)}) async-start(), calls=%async_computation.6 | async-start | bytes 5406720 | tf_op jit(solution)/shard_map/all_gather | solution.py:167
  519.3 5.5 copy-start.5
  519.3 29.8 %all-to-all-start.1 = ((bf16[32,2,16384]{2,1,0:T(2,128)(2,1)}), bf16[32,2,16384]{2,1,0:T(2,128)(2,1)S(1)}, u32[]{:S(2)}, u32[]{:S(2)}) async-start(bf16[32,2,16384]{2,1,0:T(2,128)(2,1)} %reshape.231), calls=%async_computation.2 | async-start | bytes 4194304 | tf_op jit(solution)/shard_map/all_to_all | solution.py:112
  524.8 86.5 %all-gather.13.cloned.1.call-start = ((), (), s32[]{:S(2)}) async-start(), calls=%async_computation.9 | async-start | bytes 1310720 | tf_op jit(solution)/shard_map/all_gather | solution.py:102
  525.6 288.6 %reduce-scatter.5.cloned.1.call-start = ((), (), s32[]{:S(2)}) async-start(), calls=%async_computation.8 | async-start | bytes 5406720 | tf_op jit(solution)/shard_map/reduce_scatter | solution.py:175
  617.2 198.1 %copy-start = (bf16[40,2048]{1,0:T(8,128)(2,1)S(1)}, bf16[40,2048]{1,0:T(8,128)(2,1)}, u32[]{:S(2)}) copy-start(bf16[40,2048]{1,0:T(8,128)(2,1)} %fusion.33) | copy-start | bytes 491524
  617.2 198.1 %copy-start.8 = (f32[2048]{0:T(1024)S(1)}, f32[2048]{0:T(1024)}, u32[]{:S(2)}) copy-start(f32[2048]{0:T(1024)} %param.18) | copy-start | bytes 24580
Sparse Core Ops, SparseCore 0:
  11.3 92.4 all-gather.6
  298.6 198.4 reduce-scatter.2
Sparse Core Ops, SparseCore 1:
  300.6 31.5 all-gather.10
  500.0 91.9 all-gather.8
  593.5 17.7 all-gather.12
  617.3 196.9 reduce-scatter.4
